TPU v7x, 32 devices: a whole 2x2x4 slice. The times are simulated.
32 devices in a mesh: left: 8 (over y, x, core), right: 4 (over z).
Axes of the slice: x: 2, y: 2, z: 4, core: 2. Of those that a mesh axis runs over, the one named last changes fastest.
Arguments:
- left_freq: float32 [16384], P('left'), as said below
- right_freq: float32 [16384], P('right'), as said below
- left_dirs: float32 [16, 16384], P(None, 'left'), may hold values from -6 to 6
- left_data: float32 [16, 16384], P(None, 'left'), may hold values from -6 to 6
- right_dirs: float32 [16, 16384], P(None, 'right'), may hold values from -6 to 6
- right_data: float32 [16, 16384], P(None, 'right'), may hold values from -6 to 6
- col_sketch: bfloat16 [16384, 256], P('right'), may hold values from -0.047265625 to 0.047265625
- row_sketch: bfloat16 [16384, 256], P('left'), may hold values from -0.047265625 to 0.047265625
Outputs:
- row_scaled: float32 [16384, 256], P(('left', 'right'))
- col_scaled: float32 [16384, 256], P('right')
- lower_reduced: float32 [256, 256], replicated
- shifted_reduced: float32 [256, 256], replicated
Inputs may be any that keep to these rules, and one draw needn't show every extreme that they name: left_freq[i] = 1 + (k + e) / 16384 with k distinct whole numbers of 0 to 16383 and |e| at most 0.2. right_freq[j] = 1 + (k + 0.5 + e) / 16384 with k distinct whole numbers of 0 to 16383 and |e| at most 0.2; left and right frequencies share the spacing 1 / 16384, so every left and right frequency differ by 0.1 / 16384 or more.
All inputs are finite; a program needn't handle non-finite values.
Results may differ from a plain program's by a relative error of at most 0.0089.
Values sent between devices are 32-bit elements; how exact they have to be, the bound alone decides.
A program may use at most 256 MiB of HBM per device.

v0:
```python
import math
import jax
import jax.numpy as jnp
from jax import lax
from jax.sharding import PartitionSpec as P

precise = lax.Precision.HIGHEST


def build_tiles(freq_rows, dirs_rows, data_rows, right_freq, right_dirs, right_data, total_rows):
    direct = lax.dot_general(
        data_rows,
        right_dirs,
        (((0,), (0,)), ((), ())),
        precision=precise,
        preferred_element_type=jnp.float32,
    )
    crossed = lax.dot_general(
        dirs_rows,
        right_data,
        (((0,), (0,)), ((), ())),
        precision=precise,
        preferred_element_type=jnp.float32,
    )
    spacing_gap = total_rows * (freq_rows[:, None] - right_freq[None, :])
    lower_tile = ((direct - crossed) / spacing_gap).astype(jnp.bfloat16)
    shift_tile = (
        (freq_rows[:, None] * direct - right_freq[None, :] * crossed) / spacing_gap
    ).astype(jnp.bfloat16)
    return (lower_tile, shift_tile)


def gram_of(basis):
    return lax.dot_general(
        basis,
        basis,
        (((0,), (0,)), ((), ())),
        precision=precise,
        preferred_element_type=jnp.float32,
    )


def apply_factor(basis, gram_sum, shifted_flag):
    width = gram_sum.shape[0]
    identity = jnp.eye(width, dtype=jnp.float32)
    if shifted_flag:
        gram_sum = gram_sum + 1e-05 * jnp.trace(gram_sum) / width * identity
    factor = jnp.linalg.cholesky(gram_sum)
    inverse = jax.scipy.linalg.solve_triangular(factor, identity, lower=True)
    return lax.dot_general(
        basis,
        inverse,
        (((1,), (1,)), ((), ())),
        precision=precise,
        preferred_element_type=jnp.float32,
    )


def body(
    left_freq, right_freq, left_dirs, left_data, right_dirs, right_data, col_sketch, row_sketch
):
    row_count = left_freq.shape[0]
    col_count = right_freq.shape[0]
    total_rows = row_count * lax.axis_size("left")
    total_cols = col_count * lax.axis_size("right")
    lower_tile, shift_tile = build_tiles(
        left_freq, left_dirs, left_data, right_freq, right_dirs, right_data, total_rows
    )
    row_image = lax.psum(
        jnp.dot(lower_tile, col_sketch, preferred_element_type=jnp.float32), "right"
    )
    col_image = lax.psum(
        lax.dot_general(
            lower_tile, row_sketch, (((0,), (0,)), ((), ())), preferred_element_type=jnp.float32
        ),
        "left",
    )
    row_full, col_full = (row_image, col_image)
    for sweep_index in range(2):
        gram_rows = lax.psum(gram_of(row_full), "left")
        gram_cols = lax.psum(gram_of(col_full), "right")
        row_full = apply_factor(row_full, gram_rows, sweep_index == 0)
        col_full = apply_factor(col_full, gram_cols, sweep_index == 0)
    share_rows = row_count // lax.axis_size("right")
    row_part = lax.dynamic_slice_in_dim(
        row_full, lax.axis_index("right") * share_rows, share_rows, 0
    )
    col_round = col_full.astype(jnp.bfloat16)
    lower_applied = jnp.dot(lower_tile, col_round, preferred_element_type=jnp.float32)
    shift_applied = jnp.dot(shift_tile, col_round, preferred_element_type=jnp.float32)
    lower_part = lax.dot_general(
        row_full,
        lower_applied,
        (((0,), (0,)), ((), ())),
        precision=precise,
        preferred_element_type=jnp.float32,
    )
    shift_part = lax.dot_general(
        row_full,
        shift_applied,
        (((0,), (0,)), ((), ())),
        precision=precise,
        preferred_element_type=jnp.float32,
    )
    lower_reduced, shifted_reduced = lax.psum((lower_part, shift_part), ("left", "right"))
    return (
        row_part * math.sqrt(total_rows),
        col_full * math.sqrt(total_cols),
        lower_reduced,
        shifted_reduced,
    )


def solution(mesh):
    in_specs = (
        P("left"),
        P("right"),
        P(None, "left"),
        P(None, "left"),
        P(None, "right"),
        P(None, "right"),
        P("right", None),
        P("left", None),
    )
    out_specs = (P(("left", "right"), None), P("right", None), P(), P())
    return jax.shard_map(body, mesh=mesh, in_specs=in_specs, out_specs=out_specs, check_vma=False)
```

profile of v0, /device:TPU:0, one launch (start us, length us, event | category | flops | bytes accessed | tf_op | source)
XLA Modules:
  0.0 872.8 jit_solution(7962259193701451676)
XLA Ops:
  7.3 31.2 %fusion.62 = f32[2048,4096]{1,0:T(8,128)} fusion(f32[16,2048]{1,0:T(8,128)} %param.13, f32[16,4096]{1,0:T(8,128)} %param.16), kind=kOutput, calls=%fused_computation.136 | convolution fusion | flops 1610612736 | bytes 33947648 | tf_op jit(solution)/shard_map/dot_general | solution.py:18
  38.5 40.1 %divide_convert_fusion.1 = (bf16[2048,4096]{1,0:T(8,128)(2,1)}, f32[2048,4096]{1,0:T(8,128)}) fusion(f32[2048,4096]{1,0:T(8,128)} %fusion.62, f32[4096]{0:T(1024)S(1)} %copy-done.8, f32[2048]{0:T(1024)S(1)} %copy-done.9, f32[16,2048]{1,0:T(8,128)S(1)} %copy-done.7, f32[16,4096]{1,0:T(8,128)S(1)} %copy-done.6), kind=kOutput, calls=%fused_computation.9 | convolution fusion | flops 1652555776 | bytes 84303872 | tf_op jit(solution)/shard_map/dot_general | solution.py:11
  78.6 9.6 %fusion.63 = f32[2048,256]{1,0:T(8,128)} fusion(bf16[2048,4096]{1,0:T(8,128)(2,1)} %get-tuple-element.96, bf16[4096,256]{1,0:T(8,128)(2,1)S(1)} %copy-done), kind=kOutput, calls=%fused_computation.137 | convolution fusion | flops 4294967296 | bytes 20971520 | tf_op jit(solution)/shard_map/dot_general | solution.py:70
  88.3 10.5 %fusion.66 = f32[4096,256]{1,0:T(8,128)} fusion(bf16[2048,4096]{1,0:T(8,128)(2,1)} %get-tuple-element.96, bf16[2048,256]{1,0:T(8,128)(2,1)S(1)} %copy-done.5), kind=kOutput, calls=%fused_computation.140 | convolution fusion | flops 4294967296 | bytes 22020096 | tf_op jit(solution)/shard_map/dot_general | solution.py:73
  98.8 78.8 %all-reduce.10.cloned.1.call-done = f32[2048,256]{1,0:T(8,128)} async-done(((f32[2048,256]{1,0:T(8,128)}), f32[2048,256]{1,0:T(8,128)}) %all-reduce.10.cloned.1.call-update) | async-done | bytes 2097168 | tf_op jit(solution)/shard_map/psum | solution.py:69
  184.3 52.3 %all-reduce.12.cloned.1.call-done = f32[256,256]{0,1:T(8,128)} async-done(((f32[256,256]{0,1:T(8,128)}), f32[256,256]{0,1:T(8,128)}) %all-reduce.12.cloned.1.call-update) | async-done | bytes 262160 | tf_op jit(solution)/shard_map/psum | solution.py:80
  241.0 11.7 %cholesky.214 = f32[128,128]{1,0:T(8,128)S(1)} custom-call(f32[128,128]{1,0:T(8,128)S(1)} %cholesky.346), custom_call_target="Cholesky" | custom-call | tf_op jit(solution)/shard_map/jit(cholesky)/cholesky | solution.py:48
  252.7 9.8 %custom-call.17 = f32[1,128,128]{1,2,0:T(8,128)S(1)} custom-call(f32[1,128,128]{2,1,0:T(8,128)S(1)} %get-tuple-element.95), custom_call_target="InvertDiagBlocksLowerTriangular" | custom-call | tf_op jit(solution)/shard_map/jit(cholesky)/cholesky | solution.py:48
  263.1 11.7 %cholesky.231 = f32[128,128]{1,0:T(8,128)S(1)} custom-call(f32[128,128]{1,0:T(8,128)S(1)} %convolution_subtract_fusion.7), custom_call_target="Cholesky" | custom-call | tf_op jit(solution)/shard_map/jit(cholesky)/cholesky | solution.py:48
  281.1 19.7 %custom-call.18 = f32[2,128,128]{1,2,0:T(8,128)S(1)} custom-call(f32[2,128,128]{2,1,0:T(8,128)S(1)} %get-tuple-element.32), custom_call_target="InvertDiagBlocksLowerTriangular" | custom-call | tf_op jit(solution)/shard_map/jit(_solve_triangular)/triangular_solve | solution.py:49
  310.0 83.1 %all-reduce.20.cloned.1.call-done = (f32[256,256]{0,1:T(8,128)}, f32[4096,256]{1,0:T(8,128)}) async-done(((f32[256,256]{0,1:T(8,128)}, f32[4096,256]{1,0:T(8,128)}), (f32[256,256]{0,1:T(8,128)}, f32[4096,256]{1,0:T(8,128)})) %all-reduce.20.cloned.1.call-update) | async-done | bytes 4456464 | tf_op jit(solution)/shard_map/psum | solution.py:80
  395.2 11.7 %cholesky.248 = f32[128,128]{1,0:T(8,128)S(1)} custom-call(f32[128,128]{1,0:T(8,128)S(1)} %cholesky.349), custom_call_target="Cholesky" | custom-call | tf_op jit(solution)/shard_map/jit(cholesky)/cholesky | solution.py:48
  407.6 9.8 %custom-call.19 = f32[1,128,128]{1,2,0:T(8,128)S(1)} custom-call(f32[1,128,128]{2,1,0:T(8,128)S(1)} %get-tuple-element.91), custom_call_target="InvertDiagBlocksLowerTriangular" | custom-call | tf_op jit(solution)/shard_map/jit(cholesky)/cholesky | solution.py:48
  417.9 11.7 %cholesky.265 = f32[128,128]{1,0:T(8,128)S(1)} custom-call(f32[128,128]{1,0:T(8,128)S(1)} %convolution_subtract_fusion.6), custom_call_target="Cholesky" | custom-call | tf_op jit(solution)/shard_map/jit(cholesky)/cholesky | solution.py:48
  435.9 19.7 %custom-call.20 = f32[2,128,128]{1,2,0:T(8,128)S(1)} custom-call(f32[2,128,128]{2,1,0:T(8,128)S(1)} %get-tuple-element.33), custom_call_target="InvertDiagBlocksLowerTriangular" | custom-call | tf_op jit(solution)/shard_map/jit(_solve_triangular)/triangular_solve | solution.py:49
  455.9 10.9 %fusion.67 = f32[256,256]{0,1:T(8,128)} fusion(f32[4096,256]{1,0:T(8,128)} %get-tuple-element.71), kind=kOutput, calls=%fused_computation.141 | convolution fusion | flops 3221225472 | bytes 4456448 | tf_op jit(solution)/shard_map/dot_general | solution.py:34
  467.8 34.5 %all-reduce.14.cloned.1.call-done = f32[256,256]{0,1:T(8,128)} async-done(((f32[256,256]{0,1:T(8,128)}), f32[256,256]{0,1:T(8,128)}) %all-reduce.14.cloned.1.call-update) | async-done | bytes 262160 | tf_op jit(solution)/shard_map/psum | solution.py:81
  506.7 11.7 %cholesky.282 = f32[128,128]{1,0:T(8,128)S(1)} custom-call(f32[128,128]{1,0:T(8,128)S(1)} %cholesky.352), custom_call_target="Cholesky" | custom-call | tf_op jit(solution)/shard_map/jit(cholesky)/cholesky | solution.py:48
  519.1 9.8 %custom-call.21 = f32[1,128,128]{1,2,0:T(8,128)S(1)} custom-call(f32[1,128,128]{2,1,0:T(8,128)S(1)} %get-tuple-element.87), custom_call_target="InvertDiagBlocksLowerTriangular" | custom-call | tf_op jit(solution)/shard_map/jit(cholesky)/cholesky | solution.py:48
  529.4 11.7 %cholesky.299 = f32[128,128]{1,0:T(8,128)S(1)} custom-call(f32[128,128]{1,0:T(8,128)S(1)} %convolution_subtract_fusion.5), custom_call_target="Cholesky" | custom-call | tf_op jit(solution)/shard_map/jit(cholesky)/cholesky | solution.py:48
  547.5 19.7 %custom-call.22 = f32[2,128,128]{1,2,0:T(8,128)S(1)} custom-call(f32[2,128,128]{2,1,0:T(8,128)S(1)} %get-tuple-element.34), custom_call_target="InvertDiagBlocksLowerTriangular" | custom-call | tf_op jit(solution)/shard_map/jit(_solve_triangular)/triangular_solve | solution.py:49
  575.5 7.4 fusion.68
  586.4 31.8 %all-reduce.16.cloned.1.call-done = f32[256,256]{0,1:T(8,128)} async-done(((f32[256,256]{0,1:T(8,128)}), f32[256,256]{0,1:T(8,128)}) %all-reduce.16.cloned.1.call-update) | async-done | bytes 262160 | tf_op jit(solution)/shard_map/psum | solution.py:81
  620.3 11.7 %cholesky.316 = f32[128,128]{1,0:T(8,128)S(1)} custom-call(f32[128,128]{1,0:T(8,128)S(1)} %cholesky.355), custom_call_target="Cholesky" | custom-call | tf_op jit(solution)/shard_map/jit(cholesky)/cholesky | solution.py:48
  632.7 9.8 %custom-call.23 = f32[1,128,128]{1,2,0:T(8,128)S(1)} custom-call(f32[1,128,128]{2,1,0:T(8,128)S(1)} %get-tuple-element.83), custom_call_target="InvertDiagBlocksLowerTriangular" | custom-call | tf_op jit(solution)/shard_map/jit(cholesky)/cholesky | solution.py:48
  643.0 11.9 %cholesky.333 = f32[128,128]{1,0:T(8,128)S(1)} custom-call(f32[128,128]{1,0:T(8,128)S(1)} %convolution_subtract_fusion.4), custom_call_target="Cholesky" | custom-call | tf_op jit(solution)/shard_map/jit(cholesky)/cholesky | solution.py:48
  660.9 19.7 %custom-call.24 = f32[2,128,128]{1,2,0:T(8,128)S(1)} custom-call(f32[2,128,128]{2,1,0:T(8,128)S(1)} %get-tuple-element.35), custom_call_target="InvertDiagBlocksLowerTriangular" | custom-call | tf_op jit(solution)/shard_map/jit(_solve_triangular)/triangular_solve | solution.py:49
  681.7 7.7 broadcast_multiply_fusion
  689.3 9.5 %fusion.2 = f32[2048,256]{1,0:T(8,128)} fusion(bf16[2048,4096]{1,0:T(8,128)(2,1)} %get-tuple-element.96, bf16[4096,256]{1,0:T(8,128)(2,1)S(1)} %get-tuple-element.107), kind=kOutput, calls=%fused_computation.22 | convolution fusion | flops 4294967296 | bytes 20971520 | tf_op jit(solution)/shard_map/dot_general | solution.py:89
  698.8 24.5 %fusion = f32[2048,256]{1,0:T(8,128)} fusion(f32[2048,4096]{1,0:T(8,128)} %fusion.62, f32[2048,4096]{1,0:T(8,128)} %get-tuple-element.97, f32[4096]{0:T(1024)S(1)} %copy-done.8, f32[2048]{0:T(1024)S(1)} %copy-done.9, bf16[4096,256]{1,0:T(8,128)(2,1)S(1)} %get-tuple-element.107), kind=kOutput, calls=%fused_computation.11 | convolution fusion | flops 4353687552 | bytes 71327744 | tf_op jit(solution)/shard_map/dot_general | solution.py:90
  723.3 6.5 fusion.69
  736.1 126.1 %all-reduce.18.cloned.1.call-done = (f32[256,256]{1,0:T(8,128)}, f32[256,256]{1,0:T(8,128)}) async-done(((f32[256,256]{1,0:T(8,128)}, f32[256,256]{1,0:T(8,128)}), (f32[256,256]{1,0:T(8,128)}, f32[256,256]{1,0:T(8,128)})) %all-reduce.18.cloned.1.call-update) | async-done | bytes 524304 | tf_op jit(solution)/shard_map/psum | solution.py:105
  (135 shorter events, 90.6 us)
Async XLA Ops:
  7.2 71.5 %copy-start = (bf16[4096,256]{1,0:T(8,128)(2,1)S(1)}, bf16[4096,256]{1,0:T(8,128)(2,1)}, u32[]{:S(2)}) copy-start(bf16[4096,256]{1,0:T(8,128)(2,1)} %param.17) | copy-start | bytes 6291460
  7.2 31.3 %copy-start.8 = (f32[4096]{0:T(1024)S(1)}, f32[4096]{0:T(1024)}, u32[]{:S(2)}) copy-start(f32[4096]{0:T(1024)} %param.12) | copy-start | bytes 49156
  7.2 31.3 %copy-start.9 = (f32[2048]{0:T(1024)S(1)}, f32[2048]{0:T(1024)}, u32[]{:S(2)}) copy-start(f32[2048]{0:T(1024)} %param.11) | copy-start | bytes 24580
  7.2 31.3 %copy-start.6 = (f32[16,4096]{1,0:T(8,128)S(1)}, f32[16,4096]{1,0:T(8,128)}, u32[]{:S(2)}) copy-start(f32[16,4096]{1,0:T(8,128)} %param.15) | copy-start | bytes 786436
  7.2 31.3 %copy-start.7 = (f32[16,2048]{1,0:T(8,128)S(1)}, f32[16,2048]{1,0:T(8,128)}, u32[]{:S(2)}) copy-start(f32[16,2048]{1,0:T(8,128)} %param.14) | copy-start | bytes 393220
  7.2 170.4 %all-reduce.10.cloned.1.call-start = ((), (), s32[]{:S(2)}) async-start(), calls=%async_computation | async-start | bytes 4194304 | tf_op jit(solution)/shard_map/psum | solution.py:69
  78.6 9.6 %copy-start.5 = (bf16[2048,256]{1,0:T(8,128)(2,1)S(1)}, bf16[2048,256]{1,0:T(8,128)(2,1)}, u32[]{:S(2)}) copy-start(bf16[2048,256]{1,0:T(8,128)(2,1)} %param.18) | copy-start | bytes 3145732
  88.2 148.4 %all-reduce.12.cloned.1.call-start = ((), (), s32[]{:S(2)}) async-start(), calls=%async_computation.1 | async-start | bytes 524288 | tf_op jit(solution)/shard_map/psum | solution.py:80
  184.0 209.1 %all-reduce.20.cloned.1.call-start = ((), (), s32[]{:S(2)}) async-start(), calls=%async_computation.5 | async-start | bytes 8912896 | tf_op jit(solution)/shard_map/psum | solution.py:80
  309.5 192.8 %all-reduce.14.cloned.1.call-start = ((), (), s32[]{:S(2)}) async-start(), calls=%async_computation.2 | async-start | bytes 524288 | tf_op jit(solution)/shard_map/psum | solution.py:81
  466.8 151.4 %all-reduce.16.cloned.1.call-start = ((), (), s32[]{:S(2)}) async-start(), calls=%async_computation.3 | async-start | bytes 524288 | tf_op jit(solution)/shard_map/psum | solution.py:81
  573.6 2.0 copy-start.2
  583.0 279.2 %all-reduce.18.cloned.1.call-start = ((), (), s32[]{:S(2)}) async-start(), calls=%async_computation.4 | async-start | bytes 1048576 | tf_op jit(solution)/shard_map/psum | solution.py:105
  723.3 6.6 copy-start.3
  723.3 6.6 copy-start.4
  723.3 142.2 %copy-start.1 = (bf16[4096,256]{1,0:T(8,128)(2,1)S(1)}, bf16[4096,256]{1,0:T(8,128)(2,1)}, u32[]{:S(2)}) copy-start(bf16[4096,256]{1,0:T(8,128)(2,1)} %param.17) | copy-start | bytes 6291460
Sparse Core Ops, SparseCore 0:
  88.3 89.1 all-reduce.9
  184.1 52.4 all-reduce.11
  309.6 83.4 all-reduce.19
  466.9 35.3 all-reduce.13
  583.1 35.0 all-reduce.15
  734.3 127.8 all-reduce.17
where the time goes:
time: 879 us; the launch traced here: 873 us
  waiting for transfers between devices  407 us (46%)
  other arithmetic  228 us (26%)
  matrix products  191 us (22%)
  local copies, waits for them, and re-layouts  23.8 us (3%)
  between operations  21.6 us (2%)
    another operation x27, other arithmetic, apply_factor(): factor = jnp.linalg.cholesky(gram_sum)  138 us
    psum x2, waiting for transfers between devices, body(): gram_rows = lax.psum(gram_of(row_full), 'left')  135 us
    psum x1, waiting for transfers between devices, body(): lax.psum((lower_part, shift_part), ('left', 'right'))  126 us
    psum x1, waiting for transfers between devices, body(): lax.psum(jnp.dot(lower_tile, col_sketch, preferred_element_type=jnp.float...  78.8 us
    another operation x9, other arithmetic, apply_factor(): inverse = jax.scipy.linalg.solve_triangular(factor, identity, lower=True)  78.8 us
    psum x2, waiting for transfers between devices, body(): gram_cols = lax.psum(gram_of(col_full), 'right')  66.4 us
    dot_general x1, matrix products, build_tiles(): lax.dot_general(data_rows, right_dirs, (((0,), (0,)), ((), ())), precisio...  40.1 us
    dot_general x1, matrix products, build_tiles(): lax.dot_general(dirs_rows, right_data, (((0,), (0,)), ((), ())), precisio...  31.2 us
  transfers between devices with their start and end apart: 6, of which 6 were waited for; matrix products, arithmetic and copies ran while one was open for 2% of the time, Pallas kernels for 0%

commit v1 on v0

--- a/solution.py
+++ b/solution.py
@@ -66,8 +66,11 @@
     lower_tile, shift_tile = build_tiles(
         left_freq, left_dirs, left_data, right_freq, right_dirs, right_data, total_rows
     )
-    row_image = lax.psum(
-        jnp.dot(lower_tile, col_sketch, preferred_element_type=jnp.float32), "right"
+    row_image = jnp.sum(
+        lax.all_gather(
+            jnp.dot(lower_tile, col_sketch, preferred_element_type=jnp.float32), "right"
+        ),
+        axis=0,
     )
     col_image = lax.psum(
         lax.dot_general(

time: 879 us -> 943 us (1.073)
  waiting for transfers between devices: 407 us -> 469 us
    all_gather x0 -> x1, waiting for transfers between devices: none -> 142 us  [body(): lax.all_gather(jnp.dot(lower_tile, col_sketch, preferred_element_type=jnp...]
    psum x1 -> x0, waiting for transfers between devices: 78.8 us -> none  [body(): lax.psum(jnp.dot(lower_tile, col_sketch, preferred_element_type=jnp.float...]
where the time goes in v1:
time: 943 us; the launch traced here: 937 us
  waiting for transfers between devices  469 us (50%)
  other arithmetic  232 us (25%)
  matrix products  188 us (20%)
  local copies, waits for them, and re-layouts  23.8 us (3%)
  between operations  21.6 us (2%)
    all_gather x1, waiting for transfers between devices, body(): lax.all_gather(jnp.dot(lower_tile, col_sketch, preferred_element_type=jnp...  142 us
    another operation x27, other arithmetic, apply_factor(): factor = jnp.linalg.cholesky(gram_sum)  138 us
    psum x2, waiting for transfers between devices, body(): gram_rows = lax.psum(gram_of(row_full), 'left')  135 us
    psum x1, waiting for transfers between devices, body(): lax.psum((lower_part, shift_part), ('left', 'right'))  126 us
    another operation x9, other arithmetic, apply_factor(): inverse = jax.scipy.linalg.solve_triangular(factor, identity, lower=True)  78.8 us
    psum x2, waiting for transfers between devices, body(): gram_cols = lax.psum(gram_of(col_full), 'right')  66.4 us
    dot_general x1, matrix products, build_tiles(): lax.dot_general(data_rows, right_dirs, (((0,), (0,)), ((), ())), precisio...  40.1 us
    dot_general x1, matrix products, build_tiles(): lax.dot_general(dirs_rows, right_data, (((0,), (0,)), ((), ())), precisio...  31.2 us
  transfers between devices with their start and end apart: 6, of which 6 were waited for; matrix products, arithmetic and copies ran while one was open for 2% of the time, Pallas kernels for 0%

profile of v1, /device:TPU:0, one launch (start us, length us, event | category | flops | bytes accessed | tf_op | source)
XLA Modules:
  0.0 937.3 jit_solution(9835891311464156900)
XLA Ops:
  7.3 31.2 %fusion.62 = f32[2048,4096]{1,0:T(8,128)} fusion(f32[16,2048]{1,0:T(8,128)} %param.13, f32[16,4096]{1,0:T(8,128)} %param.16), kind=kOutput, calls=%fused_computation.136 | convolution fusion | flops 1610612736 | bytes 33947648 | tf_op jit(solution)/shard_map/dot_general | solution.py:18
  38.5 40.1 %divide_convert_fusion.1 = (bf16[2048,4096]{1,0:T(8,128)(2,1)}, f32[2048,4096]{1,0:T(8,128)}) fusion(f32[2048,4096]{1,0:T(8,128)} %fusion.62, f32[4096]{0:T(1024)S(1)} %copy-done.9, f32[2048]{0:T(1024)S(1)} %copy-done.10, f32[16,2048]{1,0:T(8,128)S(1)} %copy-done.8, f32[16,4096]{1,0:T(8,128)S(1)} %copy-done.7), kind=kOutput, calls=%fused_computation.9 | convolution fusion | flops 1652555776 | bytes 84303872 | tf_op jit(solution)/shard_map/dot_general | solution.py:11
  78.6 9.6 %fusion.63 = f32[2048,256]{1,0:T(8,128)} fusion(bf16[2048,4096]{1,0:T(8,128)(2,1)} %get-tuple-element.96, bf16[4096,256]{1,0:T(8,128)(2,1)S(1)} %copy-done), kind=kOutput, calls=%fused_computation.137 | convolution fusion | flops 4294967296 | bytes 20971520 | tf_op jit(solution)/shard_map/dot_general | solution.py:71
  88.3 10.5 %fusion.66 = f32[4096,256]{1,0:T(8,128)} fusion(bf16[2048,4096]{1,0:T(8,128)(2,1)} %get-tuple-element.96, bf16[2048,256]{1,0:T(8,128)(2,1)S(1)} %copy-done.6), kind=kOutput, calls=%fused_computation.140 | convolution fusion | flops 4294967296 | bytes 22020096 | tf_op jit(solution)/shard_map/dot_general | solution.py:76
  98.8 142.0 %all-gather.3.cloned.1.call-done = f32[8192,256]{1,0:T(8,128)} async-done(((f32[2048,256]{1,0:T(8,128)}), f32[8192,256]{1,0:T(8,128)}) %all-gather.3.cloned.1.call-update) | async-done | bytes 8388624 | tf_op jit(solution)/shard_map/all_gather | solution.py:70
  249.4 51.6 %all-reduce.9.cloned.1.call-done = f32[256,256]{0,1:T(8,128)} async-done(((f32[256,256]{0,1:T(8,128)}), f32[256,256]{0,1:T(8,128)}) %all-reduce.9.cloned.1.call-update) | async-done | bytes 262160 | tf_op jit(solution)/shard_map/psum | solution.py:83
  305.4 11.7 %cholesky.214 = f32[128,128]{1,0:T(8,128)S(1)} custom-call(f32[128,128]{1,0:T(8,128)S(1)} %cholesky.346), custom_call_target="Cholesky" | custom-call | tf_op jit(solution)/shard_map/jit(cholesky)/cholesky | solution.py:48
  317.2 9.8 %custom-call.17 = f32[1,128,128]{1,2,0:T(8,128)S(1)} custom-call(f32[1,128,128]{2,1,0:T(8,128)S(1)} %get-tuple-element.95), custom_call_target="InvertDiagBlocksLowerTriangular" | custom-call | tf_op jit(solution)/shard_map/jit(cholesky)/cholesky | solution.py:48
  327.5 11.7 %cholesky.231 = f32[128,128]{1,0:T(8,128)S(1)} custom-call(f32[128,128]{1,0:T(8,128)S(1)} %convolution_subtract_fusion.7), custom_call_target="Cholesky" | custom-call | tf_op jit(solution)/shard_map/jit(cholesky)/cholesky | solution.py:48
  345.6 19.7 %custom-call.18 = f32[2,128,128]{1,2,0:T(8,128)S(1)} custom-call(f32[2,128,128]{2,1,0:T(8,128)S(1)} %get-tuple-element.32), custom_call_target="InvertDiagBlocksLowerTriangular" | custom-call | tf_op jit(solution)/shard_map/jit(_solve_triangular)/triangular_solve | solution.py:49
  374.4 83.1 %all-reduce.17.cloned.1.call-done = (f32[256,256]{0,1:T(8,128)}, f32[4096,256]{1,0:T(8,128)}) async-done(((f32[256,256]{0,1:T(8,128)}, f32[4096,256]{1,0:T(8,128)}), (f32[256,256]{0,1:T(8,128)}, f32[4096,256]{1,0:T(8,128)})) %all-reduce.17.cloned.1.call-update) | async-done | bytes 4456464 | tf_op jit(solution)/shard_map/psum | solution.py:83
  459.7 11.7 %cholesky.248 = f32[128,128]{1,0:T(8,128)S(1)} custom-call(f32[128,128]{1,0:T(8,128)S(1)} %cholesky.349), custom_call_target="Cholesky" | custom-call | tf_op jit(solution)/shard_map/jit(cholesky)/cholesky | solution.py:48
  472.0 9.8 %custom-call.19 = f32[1,128,128]{1,2,0:T(8,128)S(1)} custom-call(f32[1,128,128]{2,1,0:T(8,128)S(1)} %get-tuple-element.91), custom_call_target="InvertDiagBlocksLowerTriangular" | custom-call | tf_op jit(solution)/shard_map/jit(cholesky)/cholesky | solution.py:48
  482.4 11.7 %cholesky.265 = f32[128,128]{1,0:T(8,128)S(1)} custom-call(f32[128,128]{1,0:T(8,128)S(1)} %convolution_subtract_fusion.6), custom_call_target="Cholesky" | custom-call | tf_op jit(solution)/shard_map/jit(cholesky)/cholesky | solution.py:48
  500.3 19.7 %custom-call.20 = f32[2,128,128]{1,2,0:T(8,128)S(1)} custom-call(f32[2,128,128]{2,1,0:T(8,128)S(1)} %get-tuple-element.33), custom_call_target="InvertDiagBlocksLowerTriangular" | custom-call | tf_op jit(solution)/shard_map/jit(_solve_triangular)/triangular_solve | solution.py:49
  520.3 10.9 %fusion.67 = f32[256,256]{0,1:T(8,128)} fusion(f32[4096,256]{1,0:T(8,128)} %get-tuple-element.71), kind=kOutput, calls=%fused_computation.141 | convolution fusion | flops 3221225472 | bytes 4456448 | tf_op jit(solution)/shard_map/dot_general | solution.py:34
  532.2 34.6 %all-reduce.11.cloned.1.call-done = f32[256,256]{0,1:T(8,128)} async-done(((f32[256,256]{0,1:T(8,128)}), f32[256,256]{0,1:T(8,128)}) %all-reduce.11.cloned.1.call-update) | async-done | bytes 262160 | tf_op jit(solution)/shard_map/psum | solution.py:84
  571.1 11.7 %cholesky.282 = f32[128,128]{1,0:T(8,128)S(1)} custom-call(f32[128,128]{1,0:T(8,128)S(1)} %cholesky.352), custom_call_target="Cholesky" | custom-call | tf_op jit(solution)/shard_map/jit(cholesky)/cholesky | solution.py:48
  583.5 9.8 %custom-call.21 = f32[1,128,128]{1,2,0:T(8,128)S(1)} custom-call(f32[1,128,128]{2,1,0:T(8,128)S(1)} %get-tuple-element.87), custom_call_target="InvertDiagBlocksLowerTriangular" | custom-call | tf_op jit(solution)/shard_map/jit(cholesky)/cholesky | solution.py:48
  593.8 11.7 %cholesky.299 = f32[128,128]{1,0:T(8,128)S(1)} custom-call(f32[128,128]{1,0:T(8,128)S(1)} %convolution_subtract_fusion.5), custom_call_target="Cholesky" | custom-call | tf_op jit(solution)/shard_map/jit(cholesky)/cholesky | solution.py:48
  612.0 19.7 %custom-call.22 = f32[2,128,128]{1,2,0:T(8,128)S(1)} custom-call(f32[2,128,128]{2,1,0:T(8,128)S(1)} %get-tuple-element.34), custom_call_target="InvertDiagBlocksLowerTriangular" | custom-call | tf_op jit(solution)/shard_map/jit(_solve_triangular)/triangular_solve | solution.py:49
  640.0 7.4 fusion.68
  650.8 31.8 %all-reduce.13.cloned.1.call-done = f32[256,256]{0,1:T(8,128)} async-done(((f32[256,256]{0,1:T(8,128)}), f32[256,256]{0,1:T(8,128)}) %all-reduce.13.cloned.1.call-update) | async-done | bytes 262160 | tf_op jit(solution)/shard_map/psum | solution.py:84
  684.8 11.7 %cholesky.316 = f32[128,128]{1,0:T(8,128)S(1)} custom-call(f32[128,128]{1,0:T(8,128)S(1)} %cholesky.355), custom_call_target="Cholesky" | custom-call | tf_op jit(solution)/shard_map/jit(cholesky)/cholesky | solution.py:48
  697.1 9.8 %custom-call.23 = f32[1,128,128]{1,2,0:T(8,128)S(1)} custom-call(f32[1,128,128]{2,1,0:T(8,128)S(1)} %get-tuple-element.83), custom_call_target="InvertDiagBlocksLowerTriangular" | custom-call | tf_op jit(solution)/shard_map/jit(cholesky)/cholesky | solution.py:48
  707.5 11.9 %cholesky.333 = f32[128,128]{1,0:T(8,128)S(1)} custom-call(f32[128,128]{1,0:T(8,128)S(1)} %convolution_subtract_fusion.4), custom_call_target="Cholesky" | custom-call | tf_op jit(solution)/shard_map/jit(cholesky)/cholesky | solution.py:48
  725.4 19.7 %custom-call.24 = f32[2,128,128]{1,2,0:T(8,128)S(1)} custom-call(f32[2,128,128]{2,1,0:T(8,128)S(1)} %get-tuple-element.35), custom_call_target="InvertDiagBlocksLowerTriangular" | custom-call | tf_op jit(solution)/shard_map/jit(_solve_triangular)/triangular_solve | solution.py:49
  746.1 7.7 broadcast_multiply_fusion
  753.8 9.5 %fusion.2 = f32[2048,256]{1,0:T(8,128)} fusion(bf16[2048,4096]{1,0:T(8,128)(2,1)} %get-tuple-element.96, bf16[4096,256]{1,0:T(8,128)(2,1)S(1)} %get-tuple-element.107), kind=kOutput, calls=%fused_computation.22 | convolution fusion | flops 4294967296 | bytes 20971520 | tf_op jit(solution)/shard_map/dot_general | solution.py:92
  763.3 24.5 %fusion = f32[2048,256]{1,0:T(8,128)} fusion(f32[2048,4096]{1,0:T(8,128)} %fusion.62, f32[2048,4096]{1,0:T(8,128)} %get-tuple-element.97, f32[4096]{0:T(1024)S(1)} %copy-done.9, f32[2048]{0:T(1024)S(1)} %copy-done.10, bf16[4096,256]{1,0:T(8,128)(2,1)S(1)} %get-tuple-element.107), kind=kOutput, calls=%fused_computation.11 | convolution fusion | flops 4353687552 | bytes 71327744 | tf_op jit(solution)/shard_map/dot_general | solution.py:93
  787.8 6.5 fusion.69
  800.5 126.1 %all-reduce.15.cloned.1.call-done = (f32[256,256]{1,0:T(8,128)}, f32[256,256]{1,0:T(8,128)}) async-done(((f32[256,256]{1,0:T(8,128)}, f32[256,256]{1,0:T(8,128)}), (f32[256,256]{1,0:T(8,128)}, f32[256,256]{1,0:T(8,128)})) %all-reduce.15.cloned.1.call-update) | async-done | bytes 524304 | tf_op jit(solution)/shard_map/psum | solution.py:108
  (138 shorter events, 92.6 us)
Async XLA Ops:
  7.2 71.5 %copy-start = (bf16[4096,256]{1,0:T(8,128)(2,1)S(1)}, bf16[4096,256]{1,0:T(8,128)(2,1)}, u32[]{:S(2)}) copy-start(bf16[4096,256]{1,0:T(8,128)(2,1)} %param.17) | copy-start | bytes 6291460
  7.2 31.3 %copy-start.9 = (f32[4096]{0:T(1024)S(1)}, f32[4096]{0:T(1024)}, u32[]{:S(2)}) copy-start(f32[4096]{0:T(1024)} %param.12) | copy-start | bytes 49156
  7.2 31.3 %copy-start.10 = (f32[2048]{0:T(1024)S(1)}, f32[2048]{0:T(1024)}, u32[]{:S(2)}) copy-start(f32[2048]{0:T(1024)} %param.11) | copy-start | bytes 24580
  7.2 31.3 %copy-start.7 = (f32[16,4096]{1,0:T(8,128)S(1)}, f32[16,4096]{1,0:T(8,128)}, u32[]{:S(2)}) copy-start(f32[16,4096]{1,0:T(8,128)} %param.15) | copy-start | bytes 786436
  7.2 31.3 %copy-start.8 = (f32[16,2048]{1,0:T(8,128)S(1)}, f32[16,2048]{1,0:T(8,128)}, u32[]{:S(2)}) copy-start(f32[16,2048]{1,0:T(8,128)} %param.14) | copy-start | bytes 393220
  7.2 233.5 %all-gather.3.cloned.1.call-start = ((), (), s32[]{:S(2)}) async-start(), calls=%async_computation.3 | async-start | bytes 10485760 | tf_op jit(solution)/shard_map/all_gather | solution.py:70
  78.6 9.6 %copy-start.6 = (bf16[2048,256]{1,0:T(8,128)(2,1)S(1)}, bf16[2048,256]{1,0:T(8,128)(2,1)}, u32[]{:S(2)}) copy-start(bf16[2048,256]{1,0:T(8,128)(2,1)} %param.18) | copy-start | bytes 3145732
  88.2 212.8 %all-reduce.9.cloned.1.call-start = ((), (), s32[]{:S(2)}) async-start(), calls=%async_computation | async-start | bytes 524288 | tf_op jit(solution)/shard_map/psum | solution.py:83
  244.9 96.3 %copy-start.3 = (f32[2048,256]{1,0:T(8,128)}, f32[2048,256]{1,0:T(8,128)S(1)}, u32[]{:S(2)}) copy-start(f32[2048,256]{1,0:T(8,128)S(1)} %reduce_sum.25) | copy-start | bytes 6291460
  249.1 208.4 %all-reduce.17.cloned.1.call-start = ((), (), s32[]{:S(2)}) async-start(), calls=%async_computation.5 | async-start | bytes 8912896 | tf_op jit(solution)/shard_map/psum | solution.py:83
  373.9 192.8 %all-reduce.11.cloned.1.call-start = ((), (), s32[]{:S(2)}) async-start(), calls=%async_computation.1 | async-start | bytes 524288 | tf_op jit(solution)/shard_map/psum | solution.py:84
  531.2 151.5 %all-reduce.13.cloned.1.call-start = ((), (), s32[]{:S(2)}) async-start(), calls=%async_computation.2 | async-start | bytes 524288 | tf_op jit(solution)/shard_map/psum | solution.py:84
  638.0 2.0 copy-start.2
  647.4 279.2 %all-reduce.15.cloned.1.call-start = ((), (), s32[]{:S(2)}) async-start(), calls=%async_computation.4 | async-start | bytes 1048576 | tf_op jit(solution)/shard_map/psum | solution.py:108
  787.7 6.6 copy-start.4
  787.8 6.6 copy-start.5
  787.8 142.2 %copy-start.1 = (bf16[4096,256]{1,0:T(8,128)(2,1)S(1)}, bf16[4096,256]{1,0:T(8,128)(2,1)}, u32[]{:S(2)}) copy-start(bf16[4096,256]{1,0:T(8,128)(2,1)} %param.17) | copy-start | bytes 6291460
Sparse Core Ops, SparseCore 0:
  88.4 152.3 all-gather.2
  249.3 51.7 all-reduce.8
  374.1 83.4 all-reduce.16
  531.3 35.3 all-reduce.10
  647.6 35.0 all-reduce.12
  798.8 127.8 all-reduce.14
